TPU v7x, 512 devices: a whole 4x8x8 slice. The times are simulated.
512 devices in a mesh: row: 16 (over y, core), col: 8 (over z), fib: 4 (over x).
Axes of the slice: x: 4, y: 8, z: 8, core: 2. Of those that a mesh axis runs over, the one named last changes fastest.
Arguments:
- values: bfloat16 [768, 12, 128, 128], P(('row', 'col'), 'fib'), may hold values from -3 to 3
- columns: int32 [768, 12], P(('row', 'col')), may hold values from 0 to 767, as said below
- counts: int32 [768], P(('row', 'col')), may hold values from 6 to 12, as said below
Outputs:
- square: bfloat16 [768, 12, 128, 128], P(('row', 'col'), 'fib')
- traces: float32 [2], replicated
Inputs may be any that keep to these rules, and one draw needn't show every extreme that they name: Slot 0 of block row i holds i. Every slot s >= 1 of row i, used or not, holds (i + o) mod 768 with 1 <= |o| <= 6, and the columns of one row are distinct. Row i uses slots 0 to counts[i] - 1; later slots are ignored. Some row uses all 12 slots.
All inputs are finite; a program needn't handle non-finite values.
Results may differ from a plain program's by a relative error of at most 0.001.
Values may be sent and summed in bfloat16 or wider, within the bound.
A program may use at most 128 MiB of HBM per device.

v0:
```python
import jax
import jax.numpy as jnp
from jax import lax
from jax.sharding import PartitionSpec as P

BAND = 6


def padded(array, sides, width):
    for axis, dim in sides:
        size, length = (lax.axis_size(axis), array.shape[dim])
        up = [(i, (i + 1) % size) for i in range(size)]
        down = [(j, i) for i, j in up]
        last = lax.slice_in_dim(array, length - width, length, axis=dim)
        initial = lax.slice_in_dim(array, 0, width, axis=dim)
        before = lax.ppermute(last, axis, up)
        after = lax.ppermute(initial, axis, down)
        array = jnp.concatenate([before, array, after], axis=dim)
    return array


def band_product(
    left_tiles, left_keep, fetch_index, target_cols, target_keep, window, window_cols, window_counts
):
    picked = jnp.take(window, fetch_index, axis=0)
    picked_cols = jnp.take(window_cols, fetch_index, axis=0)
    picked_counts = jnp.take(window_counts, fetch_index, axis=0)
    alive_slots = lax.broadcasted_iota(jnp.int32, picked_cols.shape, 1) < picked_counts[:, None]
    matches = (picked_cols[:, None, :] == target_cols[None, :, None]) & alive_slots[:, None, :]
    matches = matches & left_keep[:, None, None] & target_keep[None, :, None]
    chosen = jnp.einsum(
        "ajs,asxy->ajxy", matches.astype(jnp.bfloat16), picked, preferred_element_type=jnp.float32
    ).astype(jnp.bfloat16)
    return jnp.einsum("axy,ajyz->jxz", left_tiles, chosen, preferred_element_type=jnp.float32)


def body(values, columns, counts):
    rows_here = values.shape[0]
    share_count = values.shape[1]
    slot_count = columns.shape[1]
    block_total = rows_here * lax.axis_size(("row", "col"))
    fib_index = lax.axis_index("fib")
    full_rows = lax.all_gather(values, "fib", axis=1, tiled=True)
    window, window_cols, window_counts = (
        padded(full_rows, ((("row", "col"), 0),), BAND),
        padded(columns, ((("row", "col"), 0),), BAND),
        padded(counts, ((("row", "col"), 0),), BAND),
    )
    local_rows = jnp.arange(rows_here, dtype=jnp.int32)
    row_ids = lax.axis_index(("row", "col")) * rows_here + local_rows
    fetch_all = (columns - row_ids[:, None] + BAND) % block_total + local_rows[:, None]
    slot_ids = jnp.arange(slot_count, dtype=jnp.int32)
    keep_mask = slot_ids[None, :] < counts[:, None]
    first_slot = fib_index * share_count

    def one_row(operands):
        left_tiles, left_keep, fetch_index, target_cols, target_keep = operands
        return band_product(
            left_tiles,
            left_keep,
            fetch_index,
            target_cols,
            target_keep,
            window,
            window_cols,
            window_counts,
        )

    left_fetch = lax.dynamic_slice_in_dim(fetch_all, first_slot, share_count, 1)
    left_keep = lax.dynamic_slice_in_dim(keep_mask, first_slot, share_count, 1)
    partial_value = lax.map(one_row, (values, left_keep, left_fetch, columns, keep_mask))
    regrouped = lax.all_to_all(partial_value[None], "fib", split_axis=2, concat_axis=0, tiled=True)
    product = jnp.sum(regrouped, axis=0)
    is_first = (fib_index == 0).astype(jnp.float32)
    trace_values = is_first * jnp.sum(
        jnp.diagonal(values[:, 0].astype(jnp.float32), axis1=1, axis2=2)
    )
    trace_square = is_first * jnp.sum(jnp.diagonal(product[:, 0], axis1=1, axis2=2))
    traces = lax.psum(jnp.stack([trace_values, trace_square]), ("row", "col", "fib"))
    return (product.astype(jnp.bfloat16), traces)


def solution(mesh):
    in_specs = (P(("row", "col"), "fib", None, None), P(("row", "col"), None), P(("row", "col")))
    out_specs = (P(("row", "col"), "fib", None, None), P())
    return jax.shard_map(body, mesh=mesh, in_specs=in_specs, out_specs=out_specs, check_vma=False)
```

profile of v0, /device:TPU:1, one launch (start us, length us, event | category | flops | bytes accessed | tf_op | source)
XLA Modules:
  0.0 354.2 jit_solution(3832877042432415155)
XLA Ops:
  7.9 45.8 %all-gather.2.cloned.1.call-done = bf16[6,12,128,128]{3,2,1,0:T(8,128)(2,1)} async-done(((bf16[6,3,128,128]{3,2,1,0:T(8,128)(2,1)}), bf16[6,12,128,128]{3,2,1,0:T(8,128)(2,1)}) %all-gather.2.cloned.1.call-update) | async-done | bytes 2359312 | tf_op jit(solution)/shard_map/all_gather | solution.py:43
  53.7 3.3 collective-permute-start.4
  57.0 5.0 %collective-permute-start.5 = (bf16[6,12,128,128]{3,2,1,0:T(8,128)(2,1)}, bf16[6,12,128,128]{3,2,1,0:T(8,128)(2,1)}, u32[]{:S(2)}, u32[]{:S(2)}) collective-permute-start(bf16[6,12,128,128]{3,2,1,0:T(8,128)(2,1)} %all-gather.2.cloned.1.call-done), channel_id=1, source_target_pairs={{4,0},{8,4},{12,8},{16,12},{20,16},{24,20},{28,24},{32,28},{36,32}... | collective-permute-start | bytes 7077896 | tf_op jit(solution)/shard_map/ppermute | solution.py:17
  61.9 1.9 collective-permute-start
  63.8 4.9 %collective-permute-start.1 = (s32[6,12]{1,0:T(8,128)}, s32[6,12]{1,0:T(8,128)S(1)}, u32[]{:S(2)}, u32[]{:S(2)}) collective-permute-start(s32[6,12]{1,0:T(8,128)} %param.6), channel_id=1, source_target_pairs={{4,0},{8,4},{12,8},{16,12},{20,16},{24,20},{28,24},{32,28},{36,32}... | collective-permute-start | bytes 872 | tf_op jit(solution)/shard_map/ppermute | solution.py:17
  68.7 1.9 collective-permute-start.2
  70.7 0.7 iota_compare_fusion.1
  71.5 0.8 fusion.18
  72.3 39.8 %collective-permute-done.2 = s32[6]{0:T(128)S(1)} collective-permute-done((s32[6]{0:T(128)}, s32[6]{0:T(128)S(1)}, u32[]{:S(2)}, u32[]{:S(2)}) %collective-permute-start.2) | collective-permute-done | bytes 56 | tf_op jit(solution)/shard_map/ppermute | solution.py:16
  112.2 2.9 collective-permute-start.3
  115.1 1.5 collective-permute-done.3
  116.6 0.7 pad_add_fusion.1
  117.3 0.7 pad_add_fusion
  118.1 5.9 %pad_maximum_fusion = bf16[18,12,128,128]{3,2,1,0:T(8,128)(2,1)} fusion(bf16[6,12,128,128]{3,2,1,0:T(8,128)(2,1)} %collective-permute-done.5, bf16[6,12,128,128]{3,2,1,0:T(8,128)(2,1)} %all-gather.2.cloned.1.call-done, bf16[6,12,128,128]{3,2,1,0:T(8,128)(2,1)S(1)} %collective-permute-done.4), kind=kLoop, calls=%fused_computation.37 | loop fusion | flops 7077888 | bytes 14155776 | tf_op jit(solution)/shard_map/concatenate | solution.py:18
  123.9 50.9 %while.10 = (s32[]{:T(128)}, f32[6,12,128,128]{2,3,0,1:T(8,128)}, s32[6,3]{1,0:T(8,128)S(1)}, s32[18,12]{1,0:T(8,128)S(1)}, s32[6,12]{1,0:T(8,128)}, /*index=5*/...) while((s32[]{:T(128)}, f32[6,12,128,128]{2,3,0,1:T(8,128)}, ...), condition=%wide.region_1.2_spmd, body=%wide.region_0.1_spmd.sunk | while | flops 166333216 | bytes 9541871 | solution.py:71
  124.6 3.8 %gather_fusion = bf16[3,12,128,128]{3,2,1,0:T(8,128)(2,1)S(1)} fusion(bf16[18,12,128,128]{3,2,1,0:T(8,128)(2,1)} %get-tuple-element.178, s32[1024]{0:T(1024)S(1)} %pad_clamp_fusion.2), kind=kCustom, calls=%fused_computation.2.clone.1 | custom fusion | bytes 2359308 | tf_op jit(solution)/shard_map/while/body/eval_jaxpr/jit(_take)/gather | solution.py:25
  129.3 0.7 fusion.31
  130.0 0.9 convolution_convert_fusion.2
  131.0 1.5 fusion.32
  133.1 3.8 %gather_fusion = bf16[3,12,128,128]{3,2,1,0:T(8,128)(2,1)S(1)} fusion(bf16[18,12,128,128]{3,2,1,0:T(8,128)(2,1)} %get-tuple-element.178, s32[1024]{0:T(1024)S(1)} %pad_clamp_fusion.2), kind=kCustom, calls=%fused_computation.2.clone.1 | custom fusion | bytes 2359308 | tf_op jit(solution)/shard_map/while/body/eval_jaxpr/jit(_take)/gather | solution.py:25
  137.8 0.7 fusion.31
  138.5 0.9 convolution_convert_fusion.2
  139.4 1.5 fusion.32
  141.6 3.8 %gather_fusion = bf16[3,12,128,128]{3,2,1,0:T(8,128)(2,1)S(1)} fusion(bf16[18,12,128,128]{3,2,1,0:T(8,128)(2,1)} %get-tuple-element.178, s32[1024]{0:T(1024)S(1)} %pad_clamp_fusion.2), kind=kCustom, calls=%fused_computation.2.clone.1 | custom fusion | bytes 2359308 | tf_op jit(solution)/shard_map/while/body/eval_jaxpr/jit(_take)/gather | solution.py:25
  146.3 0.7 fusion.31
  147.0 0.9 convolution_convert_fusion.2
  147.9 1.5 fusion.32
  150.1 3.8 %gather_fusion = bf16[3,12,128,128]{3,2,1,0:T(8,128)(2,1)S(1)} fusion(bf16[18,12,128,128]{3,2,1,0:T(8,128)(2,1)} %get-tuple-element.178, s32[1024]{0:T(1024)S(1)} %pad_clamp_fusion.2), kind=kCustom, calls=%fused_computation.2.clone.1 | custom fusion | bytes 2359308 | tf_op jit(solution)/shard_map/while/body/eval_jaxpr/jit(_take)/gather | solution.py:25
  154.8 0.7 fusion.31
  155.5 0.9 convolution_convert_fusion.2
  156.4 1.5 fusion.32
  158.5 3.8 %gather_fusion = bf16[3,12,128,128]{3,2,1,0:T(8,128)(2,1)S(1)} fusion(bf16[18,12,128,128]{3,2,1,0:T(8,128)(2,1)} %get-tuple-element.178, s32[1024]{0:T(1024)S(1)} %pad_clamp_fusion.2), kind=kCustom, calls=%fused_computation.2.clone.1 | custom fusion | bytes 2359308 | tf_op jit(solution)/shard_map/while/body/eval_jaxpr/jit(_take)/gather | solution.py:25
  163.2 0.7 fusion.31
  163.9 0.9 convolution_convert_fusion.2
  164.9 1.5 fusion.32
  167.0 3.8 %gather_fusion = bf16[3,12,128,128]{3,2,1,0:T(8,128)(2,1)S(1)} fusion(bf16[18,12,128,128]{3,2,1,0:T(8,128)(2,1)} %get-tuple-element.178, s32[1024]{0:T(1024)S(1)} %pad_clamp_fusion.2), kind=kCustom, calls=%fused_computation.2.clone.1 | custom fusion | bytes 2359308 | tf_op jit(solution)/shard_map/while/body/eval_jaxpr/jit(_take)/gather | solution.py:25
  172.4 0.9 convolution_convert_fusion.2
  173.3 1.5 fusion.32
  174.8 5.0 %all-to-all-start = ((f32[1,6,12,128,128]{3,4,1,0,2:T(8,128)}), f32[1,6,12,128,128]{3,4,1,0,2:T(8,128)}, u32[]{:S(2)}, u32[]{:S(2)}) async-start(f32[1,6,12,128,128]{3,4,1,0,2:T(8,128)} %bitcast.60), calls=%async_computation | async-start | bytes 9437184 | tf_op jit(solution)/shard_map/all_to_all | solution.py:72
  179.9 3.3 copy.13
  183.2 6.5 %bitcast_convert_fusion = f32[6,128,128]{0,2,1:T(8,128)} fusion(bf16[6,1,128,128]{0,3,2,1:T(8,128)(2,1)} %copy.13), kind=kLoop, calls=%fused_computation.38 | loop fusion | flops 98304 | bytes 589824 | tf_op jit(solution)/shard_map/convert_element_type | solution.py:76
  189.7 1.8 gather_fusion.3
  192.7 40.7 %all-to-all-done = f32[1,6,12,128,128]{3,4,1,0,2:T(8,128)} async-done(((f32[1,6,12,128,128]{3,4,1,0,2:T(8,128)}), f32[1,6,12,128,128]{3,4,1,0,2:T(8,128)}, u32[]{:S(2)}, u32[]{:S(2)}) %all-to-all-start) | async-done | bytes 4718624 | tf_op jit(solution)/shard_map/all_to_all | solution.py:72
  233.4 2.9 reduce_sum.27
  236.4 7.6 %copy.21 = f32[6,1,128,128]{0,3,2,1:T(8,128)} copy(f32[6,1,128,128]{2,3,1,0:T(8,128)S(1)} %copy.33) | data formatting | bytes 786432
  244.0 1.8 gather_fusion.4
  247.2 99.0 %psum.7 = f32[2]{0:T(128)} all-reduce(f32[2]{0:T(128)S(1)} %pad_maximum_fusion.1), channel_id=1, replica_groups=mesh['row'=16,'col'=8,'fib'=4] {'row','col','fib'}, use_global_device_ids=true, to_apply=%region_5.6 | all-reduce | flops 2 | bytes 16 | tf_op jit(solution)/shard_map/psum | solution.py:79
  346.3 1.1 copy.15
  (81 shorter events, 12.5 us)
Async XLA Ops:
  7.2 46.5 %all-gather.2.cloned.1.call-start = ((), (), s32[]{:S(2)}) async-start(), calls=%async_computation.1 | async-start | bytes 2949120 | tf_op jit(solution)/shard_map/all_gather | solution.py:43
  53.7 64.4 %collective-permute-start.4 = (bf16[6,12,128,128]{3,2,1,0:T(8,128)(2,1)}, bf16[6,12,128,128]{3,2,1,0:T(8,128)(2,1)S(1)}, u32[]{:S(2)}, u32[]{:S(2)}) collective-permute-start(bf16[6,12,128,128]{3,2,1,0:T(8,128)(2,1)} %all-gather.2.cloned.1.call-done), channel_id=1, source_target_pairs={{0,4},{4,8},{8,12},{12,16},{16,20},{20,24},{24,28},{28,32},{32,36}... | collective-permute-start | bytes 7077896 | tf_op jit(solution)/shard_map/ppermute | solution.py:16
  57.0 61.1 %collective-permute-start.5 = (bf16[6,12,128,128]{3,2,1,0:T(8,128)(2,1)}, bf16[6,12,128,128]{3,2,1,0:T(8,128)(2,1)}, u32[]{:S(2)}, u32[]{:S(2)}) collective-permute-start(bf16[6,12,128,128]{3,2,1,0:T(8,128)(2,1)} %all-gather.2.cloned.1.call-done), channel_id=1, source_target_pairs={{4,0},{8,4},{12,8},{16,12},{20,16},{24,20},{28,24},{32,28},{36,32}... | collective-permute-start | bytes 7077896 | tf_op jit(solution)/shard_map/ppermute | solution.py:17
  61.9 55.4 %collective-permute-start = (s32[6,12]{1,0:T(8,128)}, s32[6,12]{1,0:T(8,128)S(1)}, u32[]{:S(2)}, u32[]{:S(2)}) collective-permute-start(s32[6,12]{1,0:T(8,128)} %param.6), channel_id=1, source_target_pairs={{0,4},{4,8},{8,12},{12,16},{16,20},{20,24},{24,28},{28,32},{32,36}... | collective-permute-start | bytes 872 | tf_op jit(solution)/shard_map/ppermute | solution.py:16
  63.8 53.5 %collective-permute-start.1 = (s32[6,12]{1,0:T(8,128)}, s32[6,12]{1,0:T(8,128)S(1)}, u32[]{:S(2)}, u32[]{:S(2)}) collective-permute-start(s32[6,12]{1,0:T(8,128)} %param.6), channel_id=1, source_target_pairs={{4,0},{8,4},{12,8},{16,12},{20,16},{24,20},{28,24},{32,28},{36,32}... | collective-permute-start | bytes 872 | tf_op jit(solution)/shard_map/ppermute | solution.py:17
  68.7 43.5 %collective-permute-start.2 = (s32[6]{0:T(128)}, s32[6]{0:T(128)S(1)}, u32[]{:S(2)}, u32[]{:S(2)}) collective-permute-start(s32[6]{0:T(128)} %param.7), channel_id=1, source_target_pairs={{0,4},{4,8},{8,12},{12,16},{16,20},{20,24},{24,28},{28,32},{32,36}... | collective-permute-start | bytes 80 | tf_op jit(solution)/shard_map/ppermute | solution.py:16
  112.2 4.4 %collective-permute-start.3 = (s32[6]{0:T(128)}, s32[6]{0:T(128)S(1)}, u32[]{:S(2)}, u32[]{:S(2)}) collective-permute-start(s32[6]{0:T(128)} %param.7), channel_id=1, source_target_pairs={{4,0},{8,4},{12,8},{16,12},{20,16},{24,20},{28,24},{32,28},{36,32}... | collective-permute-start | bytes 80 | tf_op jit(solution)/shard_map/ppermute | solution.py:17
  118.0 5.9 %copy-start = (bf16[6,3,128,128]{3,2,1,0:T(8,128)(2,1)S(1)}, bf16[6,3,128,128]{3,2,1,0:T(8,128)(2,1)}, u32[]{:S(2)}) copy-start(bf16[6,3,128,128]{3,2,1,0:T(8,128)(2,1)} %param.5) | copy-start | bytes 1769476
  174.8 58.6 %all-to-all-start = ((f32[1,6,12,128,128]{3,4,1,0,2:T(8,128)}), f32[1,6,12,128,128]{3,4,1,0,2:T(8,128)}, u32[]{:S(2)}, u32[]{:S(2)}) async-start(f32[1,6,12,128,128]{3,4,1,0,2:T(8,128)} %bitcast.60), calls=%async_computation | async-start | bytes 9437184 | tf_op jit(solution)/shard_map/all_to_all | solution.py:72
Sparse Core Ops, SparseCore 0:
  10.1 43.5 all-gather.1
where the time goes:
time: 355 us; the launch traced here: 354 us
  waiting for transfers between devices  129 us (36%)
  blocking collectives  99 us (28%)
  local copies, waits for them, and re-layouts  50 us (14%)
  starting transfers between devices  24.9 us (7%)
  other arithmetic  21.6 us (6%)
  between operations  15.5 us (4%)
  matrix products  14.4 us (4%)
    psum x1, blocking collectives, body(): lax.psum(jnp.stack([trace_values, trace_square]), ('row', 'col', 'fib'))  99 us
    all_gather x1, waiting for transfers between devices, body(): full_rows = lax.all_gather(values, 'fib', axis=1, tiled=True)  45.8 us
    all_to_all x1, waiting for transfers between devices, body(): lax.all_to_all(partial_value[None], 'fib', split_axis=2, concat_axis=0, t...  40.7 us
    ppermute x3, waiting for transfers between devices, padded(): before = lax.ppermute(last, axis, up)  39.8 us
    gather x6, local copies, waits for them, and re-layouts, band_product(): picked = jnp.take(window, fetch_index, axis=0)  22.7 us
    ppermute x3, starting transfers between devices, padded(): after = lax.ppermute(initial, axis, down)  12.7 us
    dot_general x6, matrix products, band_product(): jnp.einsum('axy,ajyz->jxz', left_tiles, chosen, preferred_element_type=jn...  8.83 us
    unnamed x6, local copies, waits for them, and re-layouts  8.81 us
  transfers between devices with their start and end apart: 8, of which 4 were waited for; matrix products, arithmetic and copies ran while one was open for 4% of the time, Pallas kernels for 0%

commit v1 on v0

--- a/solution.py
+++ b/solution.py
@@ -76,7 +76,7 @@
         jnp.diagonal(values[:, 0].astype(jnp.float32), axis1=1, axis2=2)
     )
     trace_square = is_first * jnp.sum(jnp.diagonal(product[:, 0], axis1=1, axis2=2))
-    traces = lax.psum(jnp.stack([trace_values, trace_square]), ("row", "col", "fib"))
+    traces = lax.psum(lax.psum(jnp.stack([trace_values, trace_square]), "row"), ("col", "fib"))
     return (product.astype(jnp.bfloat16), traces)
 
 

time: 355 us -> 354 us (level)
  the two profiles are of different devices: /device:TPU:1 before, /device:TPU:32 now
where the time goes in v1:
time: 354 us; the launch traced here: 353 us
  waiting for transfers between devices  122 us (34%)
  blocking collectives  99.8 us (28%)
  local copies, waits for them, and re-layouts  50 us (14%)
  starting transfers between devices  29.9 us (8%)
  other arithmetic  21.7 us (6%)
  between operations  15.5 us (4%)
  matrix products  14.3 us (4%)
    psum x1, blocking collectives, body(): lax.psum(lax.psum(jnp.stack([trace_values, trace_square]), 'row'), ('col'...  75.5 us
    all_gather x1, waiting for transfers between devices, body(): full_rows = lax.all_gather(values, 'fib', axis=1, tiled=True)  44.8 us
    all_to_all x1, waiting for transfers between devices, body(): lax.all_to_all(partial_value[None], 'fib', split_axis=2, concat_axis=0, t...  42.2 us
    ppermute x3, waiting for transfers between devices, padded(): before = lax.ppermute(last, axis, up)  32.8 us
    psum x1, blocking collectives, body(): lax.psum(jnp.stack([trace_values, trace_square]), 'row')  24.3 us
    gather x6, local copies, waits for them, and re-layouts, band_product(): picked = jnp.take(window, fetch_index, axis=0)  22.7 us
    ppermute x3, starting transfers between devices, padded(): after = lax.ppermute(initial, axis, down)  17.4 us
    unnamed x6, local copies, waits for them, and re-layouts  8.77 us
  transfers between devices with their start and end apart: 8, of which 4 were waited for; matrix products, arithmetic and copies ran while one was open for 4% of the time, Pallas kernels for 0%

profile of v1, /device:TPU:32, one launch (start us, length us, event | category | flops | bytes accessed | tf_op | source)
XLA Modules:
  0.0 353.1 jit_solution(3038775738257660710)
XLA Ops:
  7.9 44.8 %all-gather.2.cloned.1.call-done = bf16[6,12,128,128]{3,2,1,0:T(8,128)(2,1)} async-done(((bf16[6,3,128,128]{3,2,1,0:T(8,128)(2,1)}), bf16[6,12,128,128]{3,2,1,0:T(8,128)(2,1)}) %all-gather.2.cloned.1.call-update) | async-done | bytes 2359312 | tf_op jit(solution)/shard_map/all_gather | solution.py:43
  52.7 3.5 %collective-permute-start.4 = (bf16[6,12,128,128]{3,2,1,0:T(8,128)(2,1)}, bf16[6,12,128,128]{3,2,1,0:T(8,128)(2,1)S(1)}, u32[]{:S(2)}, u32[]{:S(2)}) collective-permute-start(bf16[6,12,128,128]{3,2,1,0:T(8,128)(2,1)} %all-gather.2.cloned.1.call-done), channel_id=1, source_target_pairs={{0,4},{4,8},{8,12},{12,16},{16,20},{20,24},{24,28},{28,32},{32,36}... | collective-permute-start | bytes 7077896 | tf_op jit(solution)/shard_map/ppermute | solution.py:16
  56.2 5.3 %collective-permute-start.5 = (bf16[6,12,128,128]{3,2,1,0:T(8,128)(2,1)}, bf16[6,12,128,128]{3,2,1,0:T(8,128)(2,1)}, u32[]{:S(2)}, u32[]{:S(2)}) collective-permute-start(bf16[6,12,128,128]{3,2,1,0:T(8,128)(2,1)} %all-gather.2.cloned.1.call-done), channel_id=1, source_target_pairs={{4,0},{8,4},{12,8},{16,12},{20,16},{24,20},{28,24},{32,28},{36,32}... | collective-permute-start | bytes 7077896 | tf_op jit(solution)/shard_map/ppermute | solution.py:17
  61.6 1.9 collective-permute-start
  63.5 7.0 %collective-permute-start.1 = (s32[6,12]{1,0:T(8,128)}, s32[6,12]{1,0:T(8,128)S(1)}, u32[]{:S(2)}, u32[]{:S(2)}) collective-permute-start(s32[6,12]{1,0:T(8,128)} %param.6), channel_id=1, source_target_pairs={{4,0},{8,4},{12,8},{16,12},{20,16},{24,20},{28,24},{32,28},{36,32}... | collective-permute-start | bytes 872 | tf_op jit(solution)/shard_map/ppermute | solution.py:17
  70.5 1.9 collective-permute-start.2
  72.4 0.7 iota_compare_fusion.1
  73.2 0.8 fusion.18
  74.1 32.8 %collective-permute-done.2 = s32[6]{0:T(128)S(1)} collective-permute-done((s32[6]{0:T(128)}, s32[6]{0:T(128)S(1)}, u32[]{:S(2)}, u32[]{:S(2)}) %collective-permute-start.2) | collective-permute-done | bytes 56 | tf_op jit(solution)/shard_map/ppermute | solution.py:16
  106.9 5.1 %collective-permute-start.3 = (s32[6]{0:T(128)}, s32[6]{0:T(128)S(1)}, u32[]{:S(2)}, u32[]{:S(2)}) collective-permute-start(s32[6]{0:T(128)} %param.7), channel_id=1, source_target_pairs={{4,0},{8,4},{12,8},{16,12},{20,16},{24,20},{28,24},{32,28},{36,32}... | collective-permute-start | bytes 80 | tf_op jit(solution)/shard_map/ppermute | solution.py:17
  112.0 1.4 collective-permute-done.3
  113.4 0.7 pad_add_fusion.1
  114.2 0.7 pad_add_fusion
  114.9 5.9 %pad_maximum_fusion = bf16[18,12,128,128]{3,2,1,0:T(8,128)(2,1)} fusion(bf16[6,12,128,128]{3,2,1,0:T(8,128)(2,1)} %collective-permute-done.5, bf16[6,12,128,128]{3,2,1,0:T(8,128)(2,1)} %all-gather.2.cloned.1.call-done, bf16[6,12,128,128]{3,2,1,0:T(8,128)(2,1)S(1)} %collective-permute-done.4), kind=kLoop, calls=%fused_computation.37 | loop fusion | flops 7077888 | bytes 14155776 | tf_op jit(solution)/shard_map/concatenate | solution.py:18
  120.8 50.7 %while.10 = (s32[]{:T(128)}, f32[6,12,128,128]{2,3,0,1:T(8,128)}, s32[6,3]{1,0:T(8,128)S(1)}, s32[18,12]{1,0:T(8,128)S(1)}, s32[6,12]{1,0:T(8,128)}, /*index=5*/...) while((s32[]{:T(128)}, f32[6,12,128,128]{2,3,0,1:T(8,128)}, ...), condition=%wide.region_1.2_spmd, body=%wide.region_0.1_spmd.sunk | while | flops 166333216 | bytes 9541871 | solution.py:71
  121.5 3.8 %gather_fusion = bf16[3,12,128,128]{3,2,1,0:T(8,128)(2,1)S(1)} fusion(bf16[18,12,128,128]{3,2,1,0:T(8,128)(2,1)} %get-tuple-element.178, s32[1024]{0:T(1024)S(1)} %pad_clamp_fusion.2), kind=kCustom, calls=%fused_computation.2.clone.1 | custom fusion | bytes 2359308 | tf_op jit(solution)/shard_map/while/body/eval_jaxpr/jit(_take)/gather | solution.py:25
  126.2 0.7 fusion.31
  126.9 0.9 convolution_convert_fusion.2
  127.8 1.5 fusion.32
  130.0 3.8 %gather_fusion = bf16[3,12,128,128]{3,2,1,0:T(8,128)(2,1)S(1)} fusion(bf16[18,12,128,128]{3,2,1,0:T(8,128)(2,1)} %get-tuple-element.178, s32[1024]{0:T(1024)S(1)} %pad_clamp_fusion.2), kind=kCustom, calls=%fused_computation.2.clone.1 | custom fusion | bytes 2359308 | tf_op jit(solution)/shard_map/while/body/eval_jaxpr/jit(_take)/gather | solution.py:25
  135.4 0.9 convolution_convert_fusion.2
  136.3 1.4 fusion.32
  138.4 3.8 %gather_fusion = bf16[3,12,128,128]{3,2,1,0:T(8,128)(2,1)S(1)} fusion(bf16[18,12,128,128]{3,2,1,0:T(8,128)(2,1)} %get-tuple-element.178, s32[1024]{0:T(1024)S(1)} %pad_clamp_fusion.2), kind=kCustom, calls=%fused_computation.2.clone.1 | custom fusion | bytes 2359308 | tf_op jit(solution)/shard_map/while/body/eval_jaxpr/jit(_take)/gather | solution.py:25
  143.1 0.7 fusion.31
  143.8 0.9 convolution_convert_fusion.2
  144.7 1.5 fusion.32
  146.9 3.8 %gather_fusion = bf16[3,12,128,128]{3,2,1,0:T(8,128)(2,1)S(1)} fusion(bf16[18,12,128,128]{3,2,1,0:T(8,128)(2,1)} %get-tuple-element.178, s32[1024]{0:T(1024)S(1)} %pad_clamp_fusion.2), kind=kCustom, calls=%fused_computation.2.clone.1 | custom fusion | bytes 2359308 | tf_op jit(solution)/shard_map/while/body/eval_jaxpr/jit(_take)/gather | solution.py:25
  151.6 0.7 fusion.31
  152.3 0.9 convolution_convert_fusion.2
  153.2 1.4 fusion.32
  155.3 3.8 %gather_fusion = bf16[3,12,128,128]{3,2,1,0:T(8,128)(2,1)S(1)} fusion(bf16[18,12,128,128]{3,2,1,0:T(8,128)(2,1)} %get-tuple-element.178, s32[1024]{0:T(1024)S(1)} %pad_clamp_fusion.2), kind=kCustom, calls=%fused_computation.2.clone.1 | custom fusion | bytes 2359308 | tf_op jit(solution)/shard_map/while/body/eval_jaxpr/jit(_take)/gather | solution.py:25
  160.0 0.7 fusion.31
  160.7 0.9 convolution_convert_fusion.2
  161.6 1.5 fusion.32
  163.8 3.8 %gather_fusion = bf16[3,12,128,128]{3,2,1,0:T(8,128)(2,1)S(1)} fusion(bf16[18,12,128,128]{3,2,1,0:T(8,128)(2,1)} %get-tuple-element.178, s32[1024]{0:T(1024)S(1)} %pad_clamp_fusion.2), kind=kCustom, calls=%fused_computation.2.clone.1 | custom fusion | bytes 2359308 | tf_op jit(solution)/shard_map/while/body/eval_jaxpr/jit(_take)/gather | solution.py:25
  169.2 0.9 convolution_convert_fusion.2
  170.1 1.4 fusion.32
  171.6 5.0 %all-to-all-start = ((f32[1,6,12,128,128]{3,4,1,0,2:T(8,128)}), f32[1,6,12,128,128]{3,4,1,0,2:T(8,128)}, u32[]{:S(2)}, u32[]{:S(2)}) async-start(f32[1,6,12,128,128]{3,4,1,0,2:T(8,128)} %bitcast.60), calls=%async_computation | async-start | bytes 9437184 | tf_op jit(solution)/shard_map/all_to_all | solution.py:72
  176.6 3.3 copy.13
  180.0 6.5 %bitcast_convert_fusion = f32[6,128,128]{0,2,1:T(8,128)} fusion(bf16[6,1,128,128]{0,3,2,1:T(8,128)(2,1)} %copy.13), kind=kLoop, calls=%fused_computation.38 | loop fusion | flops 98304 | bytes 589824 | tf_op jit(solution)/shard_map/convert_element_type | solution.py:76
  186.4 1.8 gather_fusion.3
  189.5 42.2 %all-to-all-done = f32[1,6,12,128,128]{3,4,1,0,2:T(8,128)} async-done(((f32[1,6,12,128,128]{3,4,1,0,2:T(8,128)}), f32[1,6,12,128,128]{3,4,1,0,2:T(8,128)}, u32[]{:S(2)}, u32[]{:S(2)}) %all-to-all-start) | async-done | bytes 4718624 | tf_op jit(solution)/shard_map/all_to_all | solution.py:72
  231.6 2.9 reduce_sum.27
  234.6 7.6 %copy.21 = f32[6,1,128,128]{0,3,2,1:T(8,128)} copy(f32[6,1,128,128]{2,3,1,0:T(8,128)S(1)} %copy.33) | data formatting | bytes 786432
  242.2 1.8 gather_fusion.4
  245.3 24.3 %psum.14 = f32[2]{0:T(128)S(1)} all-reduce(f32[2]{0:T(128)S(1)} %pad_maximum_fusion.1), channel_id=1, replica_groups=mesh['row'=16,'col'=8,'fib'=4] {'row'}, use_global_device_ids=true, to_apply=%region_5.6 | all-reduce | flops 2 | bytes 16 | tf_op jit(solution)/shard_map/psum | solution.py:79
  269.7 75.5 %psum.15 = f32[2]{0:T(128)} all-reduce(f32[2]{0:T(128)S(1)} %psum.14), channel_id=1, replica_groups=mesh['row'=16,'col'=8,'fib'=4] {'col','fib'}, use_global_device_ids=true, to_apply=%region_6.7 | all-reduce | flops 2 | bytes 16 | tf_op jit(solution)/shard_map/psum | solution.py:79
  345.2 1.1 copy.15
  (82 shorter events, 13.2 us)
Async XLA Ops:
  7.2 45.5 %all-gather.2.cloned.1.call-start = ((), (), s32[]{:S(2)}) async-start(), calls=%async_computation.1 | async-start | bytes 2949120 | tf_op jit(solution)/shard_map/all_gather | solution.py:43
  52.7 62.2 %collective-permute-start.4 = (bf16[6,12,128,128]{3,2,1,0:T(8,128)(2,1)}, bf16[6,12,128,128]{3,2,1,0:T(8,128)(2,1)S(1)}, u32[]{:S(2)}, u32[]{:S(2)}) collective-permute-start(bf16[6,12,128,128]{3,2,1,0:T(8,128)(2,1)} %all-gather.2.cloned.1.call-done), channel_id=1, source_target_pairs={{0,4},{4,8},{8,12},{12,16},{16,20},{20,24},{24,28},{28,32},{32,36}... | collective-permute-start | bytes 7077896 | tf_op jit(solution)/shard_map/ppermute | solution.py:16
  56.2 58.7 %collective-permute-start.5 = (bf16[6,12,128,128]{3,2,1,0:T(8,128)(2,1)}, bf16[6,12,128,128]{3,2,1,0:T(8,128)(2,1)}, u32[]{:S(2)}, u32[]{:S(2)}) collective-permute-start(bf16[6,12,128,128]{3,2,1,0:T(8,128)(2,1)} %all-gather.2.cloned.1.call-done), channel_id=1, source_target_pairs={{4,0},{8,4},{12,8},{16,12},{20,16},{24,20},{28,24},{32,28},{36,32}... | collective-permute-start | bytes 7077896 | tf_op jit(solution)/shard_map/ppermute | solution.py:17
  61.6 52.6 %collective-permute-start = (s32[6,12]{1,0:T(8,128)}, s32[6,12]{1,0:T(8,128)S(1)}, u32[]{:S(2)}, u32[]{:S(2)}) collective-permute-start(s32[6,12]{1,0:T(8,128)} %param.6), channel_id=1, source_target_pairs={{0,4},{4,8},{8,12},{12,16},{16,20},{20,24},{24,28},{28,32},{32,36}... | collective-permute-start | bytes 872 | tf_op jit(solution)/shard_map/ppermute | solution.py:16
  63.5 50.7 %collective-permute-start.1 = (s32[6,12]{1,0:T(8,128)}, s32[6,12]{1,0:T(8,128)S(1)}, u32[]{:S(2)}, u32[]{:S(2)}) collective-permute-start(s32[6,12]{1,0:T(8,128)} %param.6), channel_id=1, source_target_pairs={{4,0},{8,4},{12,8},{16,12},{20,16},{24,20},{28,24},{32,28},{36,32}... | collective-permute-start | bytes 872 | tf_op jit(solution)/shard_map/ppermute | solution.py:17
  70.5 36.4 %collective-permute-start.2 = (s32[6]{0:T(128)}, s32[6]{0:T(128)S(1)}, u32[]{:S(2)}, u32[]{:S(2)}) collective-permute-start(s32[6]{0:T(128)} %param.7), channel_id=1, source_target_pairs={{0,4},{4,8},{8,12},{12,16},{16,20},{20,24},{24,28},{28,32},{32,36}... | collective-permute-start | bytes 80 | tf_op jit(solution)/shard_map/ppermute | solution.py:16
  106.9 6.5 %collective-permute-start.3 = (s32[6]{0:T(128)}, s32[6]{0:T(128)S(1)}, u32[]{:S(2)}, u32[]{:S(2)}) collective-permute-start(s32[6]{0:T(128)} %param.7), channel_id=1, source_target_pairs={{4,0},{8,4},{12,8},{16,12},{20,16},{24,20},{28,24},{32,28},{36,32}... | collective-permute-start | bytes 80 | tf_op jit(solution)/shard_map/ppermute | solution.py:17
  114.9 5.9 %copy-start = (bf16[6,3,128,128]{3,2,1,0:T(8,128)(2,1)S(1)}, bf16[6,3,128,128]{3,2,1,0:T(8,128)(2,1)}, u32[]{:S(2)}) copy-start(bf16[6,3,128,128]{3,2,1,0:T(8,128)(2,1)} %param.5) | copy-start | bytes 1769476
  171.6 60.1 %all-to-all-start = ((f32[1,6,12,128,128]{3,4,1,0,2:T(8,128)}), f32[1,6,12,128,128]{3,4,1,0,2:T(8,128)}, u32[]{:S(2)}, u32[]{:S(2)}) async-start(f32[1,6,12,128,128]{3,4,1,0,2:T(8,128)} %bitcast.60), calls=%async_computation | async-start | bytes 9437184 | tf_op jit(solution)/shard_map/all_to_all | solution.py:72
Sparse Core Ops, SparseCore 0:
  10.1 42.5 all-gather.1
